TPU v7x, 512 devices: a whole 4x4x16 slice. The times are simulated.
512 devices in a mesh: depth: 4 (over z_hi, core), plane: 128 (over x, z_lo, y).
Axes of the slice: x: 4, y: 4, z: 16 (z_hi: 2, z_lo: 8; z = z_hi * 8 + z_lo), core: 2. Of those that a mesh axis runs over, the one named last changes fastest.
Arguments:
- magnet: float32 [3, 32, 512, 1024], P(None, 'depth', 'plane'), may hold values from -1 to 1, as said below
- mask: int32 [512, 1024], P('plane'), may hold values 0 or 1
- materials: int32 [32], P('depth'), may hold values from 0 to 3
- exchange_strength: float32 [4], replicated, may hold values from 0.5 to 2
- anisotropy: float32 [4], replicated, may hold values from 0.5 to 3
- damping: float32 [4], replicated, may hold values from 0.05 to 0.6
- source_strength: float32 [4], replicated, may hold values from 0.3 to 1.5
- thermal_strength: float32 [4], replicated, may hold values from 0.5 to 2
- pivots: float32 [32, 3, 3], replicated, may hold values from -1 to 1, as said below
- lower: float32 [32, 3, 3], replicated, may hold values from -1 to 1, as said below
- upper: float32 [32, 3, 3], replicated, may hold values from -1 to 1, as said below
- noise_stream: int32 [1], replicated, may hold values from 0 to 999999
- counter: int32 [1], replicated, may hold values from 0 to 99999
Outputs:
- magnet_next: float32 [3, 32, 512, 1024], P(None, 'depth', 'plane')
- accumulation: float32 [3, 32, 512, 1024], P(None, 'depth', 'plane')
Inputs may be any that keep to these rules, and one draw needn't show every extreme that they name: `magnet`: unit vectors. `pivots`: each block has spectral norm below 0.98. `lower`: each block has spectral norm below 1. `upper`: each block has spectral norm below 1.
All inputs are finite; a program needn't handle non-finite values. No bound on the sum of `mask` on one device may be relied on, other than what follows from the above.
Results may differ from a plain program's by a relative error of at most 0.000073.
Values sent between devices are 32-bit elements; how exact they have to be, the bound alone decides.
A program may use at most 128 MiB of HBM per device.

v0:
```python
import jax
import jax.numpy as jnp
from jax import lax
from jax.sharding import PartitionSpec as P


def padded(block, sides, width, periodic):
    for axis, dim in sides:
        count = lax.axis_size(axis)
        forward = [(i, i + 1) for i in range(count - 1)]
        if periodic:
            forward.append((count - 1, 0))
        backward = [(target, source) for source, target in forward]
        low = lax.ppermute(
            lax.slice_in_dim(block, block.shape[dim] - width, None, axis=dim), axis, forward
        )
        high = lax.ppermute(lax.slice_in_dim(block, 0, width, axis=dim), axis, backward)
        block = jnp.concatenate([low, block, high], axis=dim)
    return block


def cross(a, b):
    return jnp.stack(
        [a[1] * b[2] - a[2] * b[1], a[2] * b[0] - a[0] * b[2], a[0] * b[1] - a[1] * b[0]]
    )


def apply_block(block, vec):
    return jnp.stack(
        [
            block[row, 0] * vec[0] + block[row, 1] * vec[1] + block[row, 2] * vec[2]
            for row in range(3)
        ]
    )


def forward_sweep(source, pivots, lower, initial):
    previous = initial
    values = []
    for layer_pos in range(source.shape[1]):
        previous = apply_block(
            pivots[layer_pos], source[:, layer_pos] - apply_block(lower[layer_pos], previous)
        )
        values.append(previous)
    return values


def backward_sweep(values, upper, initial):
    after = initial
    solved = [None] * len(values)
    for layer_pos in range(len(values) - 1, -1, -1):
        after = values[layer_pos] - apply_block(upper[layer_pos], after)
        solved[layer_pos] = after
    return solved


def solve_columns(source, pivots, lower, upper):
    zero_state = jnp.zeros_like(source[:, 0])
    values = forward_sweep(source, pivots, lower, zero_state)
    return jnp.stack(backward_sweep(values, upper, zero_state), axis=1)


def hash_uniform(index, stream, counter):
    mixed = index * 739982445 + stream * 695872825 + counter * 1597334677
    mixed = mixed ^ lax.shift_right_logical(mixed, jnp.int32(16))
    mixed = mixed * 739982445
    mixed = mixed ^ lax.shift_right_logical(mixed, jnp.int32(15))
    mixed = mixed * 695872825
    mixed = mixed ^ lax.shift_right_logical(mixed, jnp.int32(16))
    return (mixed & 65535).astype(jnp.float32) / 32767.5 - 1.0


def layer_values(materials, table):
    onehot = (materials[:, None] == jnp.arange(table.shape[0], dtype=jnp.int32)[None, :]).astype(
        jnp.float32
    )
    return jnp.sum(onehot * table[None, :], axis=1)[None, :, None, None]


def normalize(vec):
    return vec / jnp.sqrt(jnp.sum(vec * vec, axis=0, keepdims=True))


def spin_solve(source, pivots, lower, upper):
    columns = lax.all_to_all(source, "depth", split_axis=3, concat_axis=1, tiled=True)
    solved = solve_columns(columns, pivots, lower, upper)
    return lax.all_to_all(solved, "depth", split_axis=1, concat_axis=3, tiled=True)


def local(
    magnet,
    mask,
    materials,
    exchange_strength,
    anisotropy,
    damping,
    source_strength,
    thermal_strength,
    pivots,
    lower,
    upper,
    noise_stream,
    counter,
):
    depth_local = magnet.shape[1]
    row_local = magnet.shape[2]
    width_y = magnet.shape[3]
    total_layers = depth_local * lax.axis_size("depth")
    total_rows = row_local * lax.axis_size("plane")
    maskf = mask.astype(jnp.float32)[None, None]
    stiff = layer_values(materials, exchange_strength)
    aniso = layer_values(materials, anisotropy)
    alpha = layer_values(materials, damping)
    beta = layer_values(materials, source_strength)
    theta = layer_values(materials, thermal_strength)
    comp = jnp.arange(3, dtype=jnp.int32)[:, None, None, None]
    layer = (lax.axis_index("depth") * depth_local + jnp.arange(depth_local, dtype=jnp.int32))[
        None, :, None, None
    ]
    xrow = (lax.axis_index("plane") * row_local + jnp.arange(row_local, dtype=jnp.int32))[
        None, None, :, None
    ]
    ycol = jnp.arange(width_y, dtype=jnp.int32)[None, None, None, :]
    index = ((comp * total_layers + layer) * total_rows + xrow) * width_y + ycol
    noise = theta * hash_uniform(index, noise_stream[0], counter[0])
    axis_z = jnp.array([0.0, 0.0, 1.0], dtype=jnp.float32)[:, None, None, None]

    def rate(field):
        masked = field * maskf
        wide = padded(masked, (("plane", 2),), 2, True)
        near = (
            wide[:, :, 3 : row_local + 3]
            + wide[:, :, 1 : row_local + 1]
            + jnp.roll(masked, 1, 3)
            + jnp.roll(masked, -1, 3)
        )
        far = (
            wide[:, :, 4 : row_local + 4]
            + wide[:, :, 0:row_local]
            + jnp.roll(masked, 2, 3)
            + jnp.roll(masked, -2, 3)
        )
        planar = 4.0 / 3.0 * near - 1.0 / 12.0 * far
        stacked = padded(masked, (("depth", 1),), 1, False)
        vertical = stacked[:, 2:] + stacked[:, :-2]
        accum = spin_solve(beta * field, pivots, lower, upper)
        heff = stiff * (planar + 0.5 * vertical) + aniso * field * axis_z + noise + 0.5 * accum
        torque = cross(field, heff)
        change = -(torque + alpha * cross(field, torque)) / (1.0 + alpha * alpha) * maskf
        return (change, accum)

    first, _ = rate(magnet)
    middle = normalize(magnet + 0.03 * first)
    second, accum = rate(middle)
    magnet_next = normalize(magnet + 0.015 * (first + second))
    return (magnet_next, accum)


def solution(mesh):
    placed = (
        P(None, "depth", "plane", None),
        P("plane", None),
        P("depth"),
        P(),
        P(),
        P(),
        P(),
        P(),
        P(),
        P(),
        P(),
        P(),
        P(),
    )
    return jax.shard_map(
        local,
        mesh=mesh,
        in_specs=placed,
        out_specs=(P(None, "depth", "plane", None), P(None, "depth", "plane", None)),
        check_vma=False,
    )
```

profile of v0, /device:TPU:3, one launch (start us, length us, event | category | flops | bytes accessed | tf_op | source)
XLA Modules:
  0.0 1313.8 jit_solution(13437907100284906902)
XLA Ops:
  8.7 9.2 reshape.5395
  17.9 15.8 %all-to-all-start = ((f32[4,1,24576]{2,1,0:T(1,128)}), f32[4,1,24576]{2,1,0:T(1,128)S(1)}, u32[]{:S(2)}, u32[]{:S(2)}) async-start(f32[4,1,24576]{2,1,0:T(1,128)} %reshape.5395), calls=%async_computation | async-start | bytes 786432 | tf_op jit(solution)/shard_map/all_to_all | solution.py:85
  34.4 7.8 collective-permute-start
  47.0 12.7 collective-permute-start.3
  113.4 10.3 reshape.5396
  174.2 7.6 multiply_add_fusion.531
  185.8 7.6 multiply_add_fusion.525
  197.2 7.8 multiply_add_fusion.519
  231.3 7.6 multiply_add_fusion.501
  254.0 7.6 multiply_add_fusion.489
  265.4 7.6 multiply_add_fusion.483
  366.5 7.6 multiply_add_fusion.429
  664.1 19.8 %all-to-all-done.1 = f32[3,32,4,256]{3,2,0,1:T(4,128)S(1)} async-done(((f32[3,32,4,256]{3,2,0,1:T(4,128)}), f32[3,32,4,256]{3,2,0,1:T(4,128)S(1)}, u32[]{:S(2)}, u32[]{:S(2)}) %all-to-all-start.1) | async-done | bytes 393248 | tf_op jit(solution)/shard_map/all_to_all | solution.py:87
  691.3 9.2 reshape.5397
  705.5 17.5 %collective-permute-start.4 = (f32[3,8,2,1024]{3,1,2,0:T(8,128)}, f32[3,8,2,1024]{3,1,2,0:T(8,128)}, u32[]{:S(2)}, u32[]{:S(2)}) collective-permute-start(f32[3,8,2,1024]{3,1,2,0:T(8,128)} %get-tuple-element.415), channel_id=1, source_target_pairs={{1,0},{2,1},{3,2},{4,3},{5,4},{6,5},{7,6},{8,7},{9,8},{10,9},{11,1... | collective-permute-start | bytes 589832 | tf_op jit(solution)/shard_map/ppermute | solution.py:17
  726.9 10.3 reshape.5398
  787.5 7.6 multiply_add_fusion.252
  799.2 7.6 multiply_add_fusion.246
  810.6 7.8 multiply_add_fusion.240
  844.7 7.6 multiply_add_fusion.222
  867.3 7.6 multiply_add_fusion.210
  878.7 7.6 multiply_add_fusion.204
  1272.9 12.3 all-to-all-start.3
  1287.8 12.4 collective-permute-start.7
  (524 shorter events, 1060.6 us)
Async XLA Ops:
  2.8 660.3 %copy-start.10 = (f32[8]{0:T(128)}, f32[8]{0:T(128)S(1)}, u32[]{:S(2)}) copy-start(f32[8]{0:T(128)S(1)} %get-tuple-element.104) | copy-start | bytes 100
  4.0 55.7 %copy-start.1 = (f32[32,3,3]{0,2,1:T(4,128)S(1)}, f32[32,3,3]{0,2,1:T(4,128)}, u32[]{:S(2)}) copy-start(f32[32,3,3]{0,2,1:T(4,128)} %param.23) | copy-start | bytes 3460
  4.0 56.2 %copy-start.2 = (f32[32,3,3]{0,2,1:T(4,128)S(1)}, f32[32,3,3]{0,2,1:T(4,128)}, u32[]{:S(2)}) copy-start(f32[32,3,3]{0,2,1:T(4,128)} %param.22) | copy-start | bytes 3460
  4.0 56.7 %copy-start.3 = (f32[32,3,3]{0,2,1:T(4,128)S(1)}, f32[32,3,3]{0,2,1:T(4,128)}, u32[]{:S(2)}) copy-start(f32[32,3,3]{0,2,1:T(4,128)} %param.24) | copy-start | bytes 3460
  17.9 93.2 %all-to-all-start = ((f32[4,1,24576]{2,1,0:T(1,128)}), f32[4,1,24576]{2,1,0:T(1,128)S(1)}, u32[]{:S(2)}, u32[]{:S(2)}) async-start(f32[4,1,24576]{2,1,0:T(1,128)} %reshape.5395), calls=%async_computation | async-start | bytes 786432 | tf_op jit(solution)/shard_map/all_to_all | solution.py:85
  34.4 649.6 %collective-permute-start = (f32[3,8,2,1024]{3,1,2,0:T(8,128)}, f32[3,8,2,1024]{3,1,2,0:T(8,128)S(1)}, u32[]{:S(2)}, u32[]{:S(2)}) collective-permute-start(f32[3,8,2,1024]{3,1,2,0:T(8,128)} %get-tuple-element.427), channel_id=1, source_target_pairs={{1,0},{2,1},{3,2},{4,3},{5,4},{6,5},{7,6},{8,7},{9,8},{10,9},{11,1... | collective-permute-start | bytes 589832 | tf_op jit(solution)/shard_map/ppermute | solution.py:17
  42.2 641.8 %collective-permute-start.1 = (f32[3,8,2,1024]{3,1,2,0:T(8,128)}, f32[3,8,2,1024]{3,1,2,0:T(8,128)}, u32[]{:S(2)}, u32[]{:S(2)}) collective-permute-start(f32[3,8,2,1024]{3,1,2,0:T(8,128)} %get-tuple-element.428), channel_id=1, source_target_pairs={{0,1},{1,2},{2,3},{3,4},{4,5},{5,6},{6,7},{7,8},{8,9},{9,10},{10,1... | collective-permute-start | bytes 589832 | tf_op jit(solution)/shard_map/ppermute | solution.py:14
  44.8 639.1 %collective-permute-start.2 = (f32[3,1,4,1024]{3,1,2,0:T(1,128)}, f32[3,1,4,1024]{3,1,2,0:T(1,128)}, u32[]{:S(2)}, u32[]{:S(2)}) collective-permute-start(f32[3,1,4,1024]{3,1,2,0:T(1,128)} %get-tuple-element.425), channel_id=1, source_target_pairs={{128,0},{256,128},{384,256},{129,1},{257,129},{385,257},{130,2},{2... | collective-permute-start | bytes 147464 | tf_op jit(solution)/shard_map/ppermute | solution.py:17
  47.0 636.9 %collective-permute-start.3 = (f32[3,1,4,1024]{3,1,2,0:T(1,128)}, f32[3,1,4,1024]{3,1,2,0:T(1,128)}, u32[]{:S(2)}, u32[]{:S(2)}) collective-permute-start(f32[3,1,4,1024]{3,1,2,0:T(1,128)} %get-tuple-element.426), channel_id=1, source_target_pairs={{0,128},{128,256},{256,384},{1,129},{129,257},{257,385},{2,130},{1... | collective-permute-start | bytes 147464 | tf_op jit(solution)/shard_map/ppermute | solution.py:14
  104.6 24.5 %copy-start.8 = (f32[3]{0:T(128)}, f32[3]{0:T(128)S(1)}, u32[]{:S(2)}) copy-start(f32[3]{0:T(128)S(1)} %maximum_maximum_fusion.1) | copy-start | bytes 40
  104.7 554.0 %copy-start.4 = (f32[3]{0:T(128)}, f32[3]{0:T(128)S(1)}, u32[]{:S(2)}) copy-start(f32[3]{0:T(128)S(1)} %maximum_maximum_fusion) | copy-start | bytes 40
  366.4 317.6 %copy-start = (f32[3,8,4,1024]{3,2,1,0:T(4,128)S(1)}, f32[3,8,4,1024]{3,2,1,0:T(4,128)}, u32[]{:S(2)}) copy-start(f32[3,8,4,1024]{3,2,1,0:T(4,128)} %param.14) | copy-start | bytes 1179652
  659.6 24.3 %all-to-all-start.1 = ((f32[3,32,4,256]{3,2,0,1:T(4,128)}), f32[3,32,4,256]{3,2,0,1:T(4,128)S(1)}, u32[]{:S(2)}, u32[]{:S(2)}) async-start(f32[3,32,4,256]{3,2,0,1:T(4,128)} %copy.279), calls=%async_computation.1 | async-start | bytes 786432 | tf_op jit(solution)/shard_map/all_to_all | solution.py:87
  683.9 2.5 copy-start.7
  700.5 24.6 %all-to-all-start.2 = ((f32[4,1,24576]{2,1,0:T(1,128)}), f32[4,1,24576]{2,1,0:T(1,128)S(1)}, u32[]{:S(2)}, u32[]{:S(2)}) async-start(f32[4,1,24576]{2,1,0:T(1,128)} %reshape.5397), calls=%async_computation.2 | async-start | bytes 786432 | tf_op jit(solution)/shard_map/all_to_all | solution.py:85
  705.5 604.6 %collective-permute-start.4 = (f32[3,8,2,1024]{3,1,2,0:T(8,128)}, f32[3,8,2,1024]{3,1,2,0:T(8,128)}, u32[]{:S(2)}, u32[]{:S(2)}) collective-permute-start(f32[3,8,2,1024]{3,1,2,0:T(8,128)} %get-tuple-element.415), channel_id=1, source_target_pairs={{1,0},{2,1},{3,2},{4,3},{5,4},{6,5},{7,6},{8,7},{9,8},{10,9},{11,1... | collective-permute-start | bytes 589832 | tf_op jit(solution)/shard_map/ppermute | solution.py:17
  723.0 587.1 %collective-permute-start.5 = (f32[3,8,2,1024]{3,1,2,0:T(8,128)}, f32[3,8,2,1024]{3,1,2,0:T(8,128)}, u32[]{:S(2)}, u32[]{:S(2)}) collective-permute-start(f32[3,8,2,1024]{3,1,2,0:T(8,128)} %get-tuple-element.416), channel_id=1, source_target_pairs={{0,1},{1,2},{2,3},{3,4},{4,5},{5,6},{6,7},{7,8},{8,9},{9,10},{10,1... | collective-permute-start | bytes 589832 | tf_op jit(solution)/shard_map/ppermute | solution.py:14
  726.9 15.6 %copy-start.9 = (f32[3]{0:T(128)S(1)}, f32[3]{0:T(128)}, u32[]{:S(2)}) copy-start(f32[3]{0:T(128)} %copy-done.8) | copy-start | bytes 40
  737.1 360.8 %copy-start.5 = (f32[3]{0:T(128)S(1)}, f32[3]{0:T(128)}, u32[]{:S(2)}) copy-start(f32[3]{0:T(128)} %copy-done.4) | copy-start | bytes 40
  1272.9 29.0 %all-to-all-start.3 = ((f32[3,32,4,256]{3,2,0,1:T(4,128)}), f32[3,32,4,256]{3,2,0,1:T(4,128)S(1)}, u32[]{:S(2)}, u32[]{:S(2)}) async-start(f32[3,32,4,256]{3,2,0,1:T(4,128)} %copy.319), calls=%async_computation.3 | async-start | bytes 786432 | tf_op jit(solution)/shard_map/all_to_all | solution.py:87
  1285.9 24.2 %collective-permute-start.6 = (f32[3,1,4,1024]{3,1,2,0:T(1,128)}, f32[3,1,4,1024]{3,1,2,0:T(1,128)}, u32[]{:S(2)}, u32[]{:S(2)}) collective-permute-start(f32[3,1,4,1024]{3,1,2,0:T(1,128)} %get-tuple-element.413), channel_id=1, source_target_pairs={{128,0},{256,128},{384,256},{129,1},{257,129},{385,257},{130,2},{2... | collective-permute-start | bytes 147464 | tf_op jit(solution)/shard_map/ppermute | solution.py:17
  1287.8 22.3 %collective-permute-start.7 = (f32[3,1,4,1024]{3,1,2,0:T(1,128)}, f32[3,1,4,1024]{3,1,2,0:T(1,128)}, u32[]{:S(2)}, u32[]{:S(2)}) collective-permute-start(f32[3,1,4,1024]{3,1,2,0:T(1,128)} %get-tuple-element.414), channel_id=1, source_target_pairs={{0,128},{128,256},{256,384},{1,129},{129,257},{257,385},{2,130},{1... | collective-permute-start | bytes 147464 | tf_op jit(solution)/shard_map/ppermute | solution.py:14
  1301.9 10.2 copy-start.12
  1301.9 10.2 copy-start.14
  (3 other events, 5.5 us)
where the time goes:
time: 1330 us; the launch traced here: 1310 us
  other arithmetic  1070 us (80%)
  local copies, waits for them, and re-layouts  106 us (8%)
  starting transfers between devices  94.2 us (7%)
  waiting for transfers between devices  26.9 us (2%)
  between operations  16.5 us (1%)
    add x186, other arithmetic, apply_block(): block[row, 0] * vec[0] + block[row, 1] * vec[1] + block[row, 2] * vec[2]  1040 us
    unnamed x36, local copies, waits for them, and re-layouts  41 us
    slice x49, local copies, waits for them, and re-layouts, apply_block(): block[row, 0] * vec[0] + block[row, 1] * vec[1] + block[row, 2] * vec[2]  34.9 us
    ppermute x4, starting transfers between devices, padded(): lax.ppermute(lax.slice_in_dim(block, 0, width, axis=dim), axis, backward)  29.4 us
    ppermute x4, starting transfers between devices, padded(): lax.ppermute(lax.slice_in_dim(block, block.shape[dim] - width, None, axis...  29.1 us
  transfers between devices with their start and end apart: 12, of which 2 were waited for; matrix products, arithmetic and copies ran while one was open for 87% of the time, Pallas kernels for 0%

commit v1 on v0

--- a/solution.py
+++ b/solution.py
@@ -82,7 +82,10 @@
 
 
 def spin_solve(source, pivots, lower, upper):
-    columns = lax.all_to_all(source, "depth", split_axis=3, concat_axis=1, tiled=True)
+    columns = jnp.concatenate(
+        lax.all_to_all(jnp.stack(jnp.split(source, lax.axis_size("depth"), axis=3)), "depth", 0, 0),
+        axis=1,
+    )
     solved = solve_columns(columns, pivots, lower, upper)
     return lax.all_to_all(solved, "depth", split_axis=1, concat_axis=3, tiled=True)
 

time: 1330 us -> 1270 us (0.955)
  local copies, waits for them, and re-layouts: 106 us -> 52.9 us
    unnamed x36 -> x72, local copies, waits for them, and re-layouts: 41 us -> 7.87 us
  transfers between devices with their start and end apart: 12 -> 12, of which waited for: 2 -> 2; matrix products, arithmetic and copies ran while one was open for 87% -> 88% of each run, Pallas kernels for 0% -> 0%
where the time goes in v1:
time: 1270 us; the launch traced here: 1260 us
  other arithmetic  1070 us (84%)
  starting transfers between devices  93.7 us (7%)
  local copies, waits for them, and re-layouts  52.9 us (4%)
  waiting for transfers between devices  26.9 us (2%)
  between operations  16.8 us (1%)
    add x186, other arithmetic, apply_block(): block[row, 0] * vec[0] + block[row, 1] * vec[1] + block[row, 2] * vec[2]  1040 us
    slice x49, local copies, waits for them, and re-layouts, apply_block(): block[row, 0] * vec[0] + block[row, 1] * vec[1] + block[row, 2] * vec[2]  34.6 us
    ppermute x4, starting transfers between devices, padded(): lax.ppermute(lax.slice_in_dim(block, 0, width, axis=dim), axis, backward)  29.4 us
    ppermute x4, starting transfers between devices, padded(): lax.ppermute(lax.slice_in_dim(block, block.shape[dim] - width, None, axis...  28.5 us
  transfers between devices with their start and end apart: 12, of which 2 were waited for; matrix products, arithmetic and copies ran while one was open for 88% of the time, Pallas kernels for 0%

profile of v1, /device:TPU:3, one launch (start us, length us, event | category | flops | bytes accessed | tf_op | source)
XLA Modules:
  0.0 1256.7 jit_solution(18408663036213584316)
XLA Ops:
  4.8 15.8 %all-to-all-start = ((f32[4,3,8,4,256]{4,2,3,1,0:T(8,128)}), f32[4,3,8,4,256]{4,2,3,1,0:T(8,128)S(1)}, u32[]{:S(2)}, u32[]{:S(2)}) async-start(f32[4,3,8,4,256]{4,2,3,1,0:T(8,128)} %pad_maximum_fusion.8), calls=%async_computation | async-start | bytes 786432 | tf_op jit(solution)/shard_map/all_to_all | solution.py:86
  21.4 7.8 collective-permute-start
  34.0 12.3 collective-permute-start.3
  98.8 7.5 multiply_add_fusion.555
  210.8 7.6 multiply_add_fusion.495
  311.2 7.6 multiply_add_fusion.441
  344.7 7.6 multiply_add_fusion.423
  356.0 7.6 multiply_add_fusion.417
  378.6 7.7 multiply_add_fusion.405
  401.6 7.6 multiply_add_fusion.393
  423.7 7.7 multiply_add_fusion.381
  435.2 7.7 multiply_add_fusion.375
  633.4 19.6 %all-to-all-done.1 = f32[3,32,4,256]{3,2,0,1:T(4,128)S(1)} async-done(((f32[3,32,4,256]{3,2,0,1:T(4,128)}), f32[3,32,4,256]{3,2,0,1:T(4,128)S(1)}, u32[]{:S(2)}, u32[]{:S(2)}) %all-to-all-start.1) | async-done | bytes 393248 | tf_op jit(solution)/shard_map/all_to_all | solution.py:90
  663.5 17.5 %collective-permute-start.4 = (f32[3,8,2,1024]{3,1,2,0:T(8,128)}, f32[3,8,2,1024]{3,1,2,0:T(8,128)}, u32[]{:S(2)}, u32[]{:S(2)}) collective-permute-start(f32[3,8,2,1024]{3,1,2,0:T(8,128)} %get-tuple-element.421), channel_id=1, source_target_pairs={{1,0},{2,1},{3,2},{4,3},{5,4},{6,5},{7,6},{8,7},{9,8},{10,9},{11,1... | collective-permute-start | bytes 589832 | tf_op jit(solution)/shard_map/ppermute | solution.py:17
  796.0 7.6 multiply_add_fusion.216
  896.4 7.6 multiply_add_fusion.162
  929.8 7.6 multiply_add_fusion.144
  941.1 7.6 multiply_add_fusion.138
  963.7 7.7 multiply_add_fusion.126
  986.7 7.6 multiply_add_fusion.114
  1008.9 7.7 multiply_add_fusion.102
  1020.3 7.7 multiply_add_fusion.96
  1214.5 12.3 all-to-all-start.3
  1229.4 12.4 collective-permute-start.7
  (559 shorter events, 1012.5 us)
Async XLA Ops:
  0.6 0.8 copy-start.30
  0.6 0.8 copy-start.34
  2.2 630.2 %copy-start.22 = (f32[8]{0:T(128)}, f32[8]{0:T(128)S(1)}, u32[]{:S(2)}) copy-start(f32[8]{0:T(128)S(1)} %get-tuple-element.106) | copy-start | bytes 100
  4.8 93.6 %all-to-all-start = ((f32[4,3,8,4,256]{4,2,3,1,0:T(8,128)}), f32[4,3,8,4,256]{4,2,3,1,0:T(8,128)S(1)}, u32[]{:S(2)}, u32[]{:S(2)}) async-start(f32[4,3,8,4,256]{4,2,3,1,0:T(8,128)} %pad_maximum_fusion.8), calls=%async_computation | async-start | bytes 786432 | tf_op jit(solution)/shard_map/all_to_all | solution.py:86
  21.4 631.8 %collective-permute-start = (f32[3,8,2,1024]{3,1,2,0:T(8,128)}, f32[3,8,2,1024]{3,1,2,0:T(8,128)S(1)}, u32[]{:S(2)}, u32[]{:S(2)}) collective-permute-start(f32[3,8,2,1024]{3,1,2,0:T(8,128)} %get-tuple-element.433), channel_id=1, source_target_pairs={{1,0},{2,1},{3,2},{4,3},{5,4},{6,5},{7,6},{8,7},{9,8},{10,9},{11,1... | collective-permute-start | bytes 589832 | tf_op jit(solution)/shard_map/ppermute | solution.py:17
  29.2 624.0 %collective-permute-start.1 = (f32[3,8,2,1024]{3,1,2,0:T(8,128)}, f32[3,8,2,1024]{3,1,2,0:T(8,128)}, u32[]{:S(2)}, u32[]{:S(2)}) collective-permute-start(f32[3,8,2,1024]{3,1,2,0:T(8,128)} %get-tuple-element.434), channel_id=1, source_target_pairs={{0,1},{1,2},{2,3},{3,4},{4,5},{5,6},{6,7},{7,8},{8,9},{9,10},{10,1... | collective-permute-start | bytes 589832 | tf_op jit(solution)/shard_map/ppermute | solution.py:14
  31.1 15.2 %copy-start.1 = (f32[32,3,3]{0,2,1:T(4,128)S(1)}, f32[32,3,3]{0,2,1:T(4,128)}, u32[]{:S(2)}) copy-start(f32[32,3,3]{0,2,1:T(4,128)} %param.23) | copy-start | bytes 3460
  31.8 621.3 %collective-permute-start.2 = (f32[3,1,4,1024]{3,1,2,0:T(1,128)}, f32[3,1,4,1024]{3,1,2,0:T(1,128)}, u32[]{:S(2)}, u32[]{:S(2)}) collective-permute-start(f32[3,1,4,1024]{3,1,2,0:T(1,128)} %get-tuple-element.431), channel_id=1, source_target_pairs={{128,0},{256,128},{384,256},{129,1},{257,129},{385,257},{130,2},{2... | collective-permute-start | bytes 147464 | tf_op jit(solution)/shard_map/ppermute | solution.py:17
  34.0 619.1 %collective-permute-start.3 = (f32[3,1,4,1024]{3,1,2,0:T(1,128)}, f32[3,1,4,1024]{3,1,2,0:T(1,128)}, u32[]{:S(2)}, u32[]{:S(2)}) collective-permute-start(f32[3,1,4,1024]{3,1,2,0:T(1,128)} %get-tuple-element.432), channel_id=1, source_target_pairs={{0,128},{128,256},{256,384},{1,129},{129,257},{257,385},{2,130},{1... | collective-permute-start | bytes 147464 | tf_op jit(solution)/shard_map/ppermute | solution.py:14
  92.0 6.8 copy-start.20
  92.1 535.8 %copy-start.10 = (f32[3]{0:T(128)}, f32[3]{0:T(128)S(1)}, u32[]{:S(2)}) copy-start(f32[3]{0:T(128)S(1)} %maximum_maximum_fusion) | copy-start | bytes 40
  628.7 24.3 %all-to-all-start.1 = ((f32[3,32,4,256]{3,2,0,1:T(4,128)}), f32[3,32,4,256]{3,2,0,1:T(4,128)S(1)}, u32[]{:S(2)}, u32[]{:S(2)}) async-start(f32[3,32,4,256]{3,2,0,1:T(4,128)} %copy.291), calls=%async_computation.1 | async-start | bytes 786432 | tf_op jit(solution)/shard_map/all_to_all | solution.py:90
  633.4 19.8 %copy-start = (f32[3,8,4,1024]{3,2,1,0:T(4,128)S(1)}, f32[3,8,4,1024]{3,2,1,0:T(4,128)}, u32[]{:S(2)}) copy-start(f32[3,8,4,1024]{3,2,1,0:T(4,128)} %param.14) | copy-start | bytes 1179652
  658.6 24.4 %all-to-all-start.2 = ((f32[4,3,8,4,256]{4,2,3,1,0:T(8,128)}), f32[4,3,8,4,256]{4,2,3,1,0:T(8,128)S(1)}, u32[]{:S(2)}, u32[]{:S(2)}) async-start(f32[4,3,8,4,256]{4,2,3,1,0:T(8,128)} %pad_maximum_fusion.9), calls=%async_computation.2 | async-start | bytes 786432 | tf_op jit(solution)/shard_map/all_to_all | solution.py:86
  663.5 588.5 %collective-permute-start.4 = (f32[3,8,2,1024]{3,1,2,0:T(8,128)}, f32[3,8,2,1024]{3,1,2,0:T(8,128)}, u32[]{:S(2)}, u32[]{:S(2)}) collective-permute-start(f32[3,8,2,1024]{3,1,2,0:T(8,128)} %get-tuple-element.421), channel_id=1, source_target_pairs={{1,0},{2,1},{3,2},{4,3},{5,4},{6,5},{7,6},{8,7},{9,8},{10,9},{11,1... | collective-permute-start | bytes 589832 | tf_op jit(solution)/shard_map/ppermute | solution.py:17
  681.0 570.9 %collective-permute-start.5 = (f32[3,8,2,1024]{3,1,2,0:T(8,128)}, f32[3,8,2,1024]{3,1,2,0:T(8,128)}, u32[]{:S(2)}, u32[]{:S(2)}) collective-permute-start(f32[3,8,2,1024]{3,1,2,0:T(8,128)} %get-tuple-element.422), channel_id=1, source_target_pairs={{0,1},{1,2},{2,3},{3,4},{4,5},{5,6},{6,7},{7,8},{8,9},{9,10},{10,1... | collective-permute-start | bytes 589832 | tf_op jit(solution)/shard_map/ppermute | solution.py:14
  1214.5 29.0 %all-to-all-start.3 = ((f32[3,32,4,256]{3,2,0,1:T(4,128)}), f32[3,32,4,256]{3,2,0,1:T(4,128)S(1)}, u32[]{:S(2)}, u32[]{:S(2)}) async-start(f32[3,32,4,256]{3,2,0,1:T(4,128)} %copy.329), calls=%async_computation.3 | async-start | bytes 786432 | tf_op jit(solution)/shard_map/all_to_all | solution.py:90
  1227.5 24.4 %collective-permute-start.6 = (f32[3,1,4,1024]{3,1,2,0:T(1,128)}, f32[3,1,4,1024]{3,1,2,0:T(1,128)}, u32[]{:S(2)}, u32[]{:S(2)}) collective-permute-start(f32[3,1,4,1024]{3,1,2,0:T(1,128)} %get-tuple-element.419), channel_id=1, source_target_pairs={{128,0},{256,128},{384,256},{129,1},{257,129},{385,257},{130,2},{2... | collective-permute-start | bytes 147464 | tf_op jit(solution)/shard_map/ppermute | solution.py:17
  1229.4 22.5 %collective-permute-start.7 = (f32[3,1,4,1024]{3,1,2,0:T(1,128)}, f32[3,1,4,1024]{3,1,2,0:T(1,128)}, u32[]{:S(2)}, u32[]{:S(2)}) collective-permute-start(f32[3,1,4,1024]{3,1,2,0:T(1,128)} %get-tuple-element.420), channel_id=1, source_target_pairs={{0,128},{128,256},{256,384},{1,129},{129,257},{257,385},{2,130},{1... | collective-permute-start | bytes 147464 | tf_op jit(solution)/shard_map/ppermute | solution.py:14
  1243.7 8.4 copy-start.4
  1243.7 8.4 copy-start.5
  1243.7 8.4 copy-start.6
  1243.7 8.4 copy-start.7
  1243.7 8.4 copy-start.26
  (23 other events, 15.7 us)
